TPU v7x, 32 devices: a whole 2x2x4 slice. The times are simulated.
32 devices in a mesh: section: 4 (over y, x), seq: 8 (over z, core).
Axes of the slice: x: 2, y: 2, z: 4, core: 2. Of those that a mesh axis runs over, the one named last changes fastest.
Arguments:
- hidden: bfloat16 [4, 1024, 2048], P('section', 'seq'), may hold values from -6 to 6
- query_gain: bfloat16 [4, 2048], P('section'), may hold values from 0.099609375 to 1.8984375
- out_gain: bfloat16 [4, 2048], P('section'), may hold values from 0.099609375 to 1.8984375
- keys_now: bfloat16 [4, 1024, 512], P('section', 'seq'), may hold values from -26.516504 to 26.516504
- values_now: bfloat16 [4, 1024, 512], P('section', 'seq'), may hold values from -6 to 6
- keys_cached: bfloat16 [4, 1024, 512], P('section', 'seq'), may hold values from -6 to 6
- values_cached: bfloat16 [4, 1024, 512], P('section', 'seq'), may hold values from -6 to 6
- first_key: int32 [4], P('section'), may hold values from 0 to 1024
Outputs:
- handoff: bfloat16 [4, 1024, 2048], P('section', 'seq')
All inputs are finite; a program needn't handle non-finite values.
Results may differ from a plain program's by a relative error of at most 0.0065.
Values may be sent and summed in bfloat16 or wider, within the bound.
A program may use at most 128 MiB of HBM per device.

v0:
```python
import math

import jax
import jax.numpy as jnp
from jax import lax
from jax.sharding import PartitionSpec as P

HEADS = 16
KV_HEADS = 4
HEAD = 128


masked_score = -1e30


def passed_along(value, axis, steps):
    count = lax.axis_size(axis)
    pairs = [(source, (source + steps) % count) for source in range(count)]
    return lax.ppermute(value, axis, pairs)


def rms_scale(values):
    return lax.rsqrt(jnp.mean(values * values, axis=-1, keepdims=True) + 1e-06)


def on_device(
    hidden, query_gain, out_gain, keys_now, values_now, keys_cached, values_cached, first_key
):
    shard_rows = hidden.shape[1]
    own_index = lax.axis_index("seq")
    seq_count = lax.axis_size("seq")
    limit = first_key[0]
    score_scale = HEAD ** (-0.5)
    head_group = HEADS // KV_HEADS
    widened = hidden[0].astype(jnp.float32)
    queries = (widened * rms_scale(widened) * query_gain[0].astype(jnp.float32)).astype(
        jnp.bfloat16
    )
    grouped = queries.reshape(shard_rows, KV_HEADS, head_group, HEAD)
    local_pos = jnp.arange(shard_rows, dtype=jnp.int32)

    def absorb(carried, key_block, value_block, usable):
        running_max, totals, weighted = carried
        scores = (
            jnp.einsum(
                "tgqd,bgd->gqtb",
                grouped,
                key_block.reshape(-1, KV_HEADS, HEAD),
                preferred_element_type=jnp.float32,
            )
            * score_scale
        )
        scores = jnp.where(usable, scores, masked_score)
        new_max = jnp.maximum(running_max, jnp.max(scores, axis=-1))
        rescale = jnp.exp(running_max - new_max)
        weights = jnp.exp(scores - new_max[..., None])
        totals = totals * rescale + jnp.sum(weights, axis=-1)
        weighted = weighted * rescale[..., None] + jnp.einsum(
            "gqtb,bgd->gqtd",
            weights.astype(jnp.bfloat16),
            value_block.reshape(-1, KV_HEADS, HEAD),
            preferred_element_type=jnp.float32,
        )
        return (new_max, totals, weighted)

    def fold_rows(carried, key_rows, value_rows, first_row):
        row_count = key_rows.shape[0]
        step_rows = math.gcd(row_count, shard_rows * max(1, 512 // shard_rows))

        def one_block(block_index, carried):
            offset = block_index * step_rows
            key_block = lax.dynamic_slice_in_dim(key_rows, offset, step_rows, 0)
            value_block = lax.dynamic_slice_in_dim(value_rows, offset, step_rows, 0)
            global_rows = first_row + offset + jnp.arange(step_rows, dtype=jnp.int32)
            source = global_rows // shard_rows
            usable = (source != own_index) & ((source < own_index) | (global_rows >= limit))
            return absorb(carried, key_block, value_block, usable)

        return lax.fori_loop(0, row_count // step_rows, one_block, carried)

    local_keys = jnp.concatenate([keys_cached[0], keys_now[0]], 0)
    local_values = jnp.concatenate([values_cached[0], values_now[0]], 0)
    earlier = (local_pos[None, :] > local_pos[:, None]) & (
        own_index * shard_rows + local_pos >= limit
    )[None, :]
    current = local_pos[None, :] <= local_pos[:, None]
    initial = (
        jnp.full((KV_HEADS, head_group, shard_rows), masked_score, jnp.float32),
        jnp.zeros((KV_HEADS, head_group, shard_rows), jnp.float32),
        jnp.zeros((KV_HEADS, head_group, shard_rows, HEAD), jnp.float32),
    )
    carried = absorb(initial, local_keys, local_values, jnp.concatenate([earlier, current], 1))
    target = jnp.arange(seq_count, dtype=jnp.int32)[:, None, None] > own_index
    outgoing_keys = jnp.where(target, keys_now[0][None], keys_cached[0][None])
    outgoing_values = jnp.where(target, values_now[0][None], values_cached[0][None])
    arrived_keys, arrived_values = (
        lax.all_to_all(outgoing_keys, "seq", split_axis=0, concat_axis=0, tiled=True),
        lax.all_to_all(outgoing_values, "seq", split_axis=0, concat_axis=0, tiled=True),
    )
    width = arrived_keys.shape[-1]
    carried = fold_rows(
        carried, arrived_keys.reshape(-1, width), arrived_values.reshape(-1, width), 0
    )
    running_max, totals, weighted = carried
    result = (weighted / totals[..., None]).astype(jnp.bfloat16)
    attended = jnp.transpose(result, (2, 0, 1, 3)).reshape(shard_rows, HEADS * HEAD)
    attended = attended.astype(jnp.float32)
    branch = attended * rms_scale(attended) * out_gain[0].astype(jnp.float32)
    layered = (widened + branch).astype(jnp.bfloat16)[None]
    return passed_along(layered, "section", 1)


def solution(mesh):
    return jax.shard_map(
        on_device,
        mesh=mesh,
        in_specs=(
            P("section", "seq", None),
            P("section", None),
            P("section", None),
            P("section", "seq", None),
            P("section", "seq", None),
            P("section", "seq", None),
            P("section", "seq", None),
            P("section"),
        ),
        out_specs=P("section", "seq", None),
        check_vma=False,
    )
```

profile of v0, /device:TPU:0, one launch (start us, length us, event | category | flops | bytes accessed | tf_op | source)
XLA Modules:
  0.0 112.4 jit_solution(16938378559292654285)
XLA Ops:
  0.0 1.1 copy.62
  1.2 1.0 copy.63
  2.2 1.0 copy.65
  3.2 1.0 copy.66
  4.3 1.6 %broadcast_select_fusion = (bf16[8,128,512]{1,2,0:T(8,128)(2,1)}, bf16[8,128,512]{1,2,0:T(8,128)(2,1)}) fusion(pred[8]{0:T(512)(128)(4,1)S(1)} %iota_compare_fusion.2, bf16[128,512]{0,1:T(8,128)(2,1)S(1)} %copy.66, bf16[128,512]{0,1:T(8,128)(2,1)S(1)} %copy.65, bf16[128,512]{0,1:T(8,128)(2,1)S(1)} %copy.63, bf16[128,512]{0,1:T(8,128)(2,1)S(1)} %copy.62), kind=kLoop, calls=%fused_computation.45 | loop fusion | flops 1048576 | bytes 2621448 | tf_op jit(solution)/shard_map/jit(_where)/select_n | solution.py:95
  5.9 6.4 %all-to-all-start = ((bf16[8,128,512]{1,2,0:T(8,128)(2,1)}), bf16[8,128,512]{1,2,0:T(8,128)(2,1)S(1)}, u32[]{:S(2)}, u32[]{:S(2)}) async-start(bf16[8,128,512]{1,2,0:T(8,128)(2,1)} %get-tuple-element.267), calls=%async_computation | async-start | bytes 2097152 | tf_op jit(solution)/shard_map/all_to_all | solution.py:97
  15.2 23.6 %all-to-all-done = bf16[8,128,512]{1,2,0:T(8,128)(2,1)S(1)} async-done(((bf16[8,128,512]{1,2,0:T(8,128)(2,1)}), bf16[8,128,512]{1,2,0:T(8,128)(2,1)S(1)}, u32[]{:S(2)}, u32[]{:S(2)}) %all-to-all-start) | async-done | bytes 1048608 | tf_op jit(solution)/shard_map/all_to_all | solution.py:97
  38.8 4.2 %all-to-all-start.1 = ((bf16[8,128,512]{1,2,0:T(8,128)(2,1)}), bf16[8,128,512]{1,2,0:T(8,128)(2,1)}, u32[]{:S(2)}, u32[]{:S(2)}) async-start(bf16[8,128,512]{1,2,0:T(8,128)(2,1)} %get-tuple-element.266), calls=%async_computation.1 | async-start | bytes 2097152 | tf_op jit(solution)/shard_map/all_to_all | solution.py:98
  44.3 1.7 %convolution_add_fusion = f32[4,4,128,128]{3,2,1,0:T(8,128)} fusion(f32[4,4,128,256]{2,3,1,0:T(8,128)S(1)} %get-tuple-element.269, f32[4,4,128]{2,1,0:T(4,128)S(1)} %broadcast_maximum_fusion, f32[4,4,128]{2,1,0:T(4,128)S(1)} %get-tuple-element.264, bf16[128,4,128]{2,0,1:T(8,128)(2,1)S(1)} %copy.60, bf16[128,4,128]{2,0,1:T(8,128)(2,1)S(1)} %copy.59), kind=kOutput, calls=%fused_computation.34 | convolution fusion | flops 136052736 | bytes 3424256 | tf_op jit(solution)/shard_map/gqtb,bgd->gqtd/dot_general | solution.py:58
  46.5 23.1 %all-to-all-done.1 = bf16[8,128,512]{1,2,0:T(8,128)(2,1)} async-done(((bf16[8,128,512]{1,2,0:T(8,128)(2,1)}), bf16[8,128,512]{1,2,0:T(8,128)(2,1)}, u32[]{:S(2)}, u32[]{:S(2)}) %all-to-all-start.1) | async-done | bytes 1048608 | tf_op jit(solution)/shard_map/all_to_all | solution.py:98
  69.6 2.3 %copy.67 = bf16[8,128,512]{2,1,0:T(8,128)(2,1)} copy(bf16[8,128,512]{1,2,0:T(8,128)(2,1)} %all-to-all-done.1) | data formatting | bytes 2097152 | tf_op jit(solution)/shard_map/all_to_all | solution.py:98
  71.9 22.2 %while.19 = (s32[]{:T(128)}, f32[4,4,128]{2,1,0:T(4,128)S(1)}, f32[4,4,128]{2,1,0:T(4,128)S(1)}, f32[4,4,128,128]{3,2,1,0:T(8,128)}, s32[]{:T(128)}, /*index=5*/...) while((s32[]{:T(128)}, f32[4,4,128]{2,1,0:T(4,128)S(1)}, ...), condition=%wide.region_6.7_spmd, body=%wide.region_3.6_spmd.sunk | while | flops 548944384 | bytes 37357784 | solution.py:79
  71.9 1.1 constant_dynamic-slice_fusion.3
  73.9 1.1 bitcast_reduce_fusion.2
  75.0 1.9 %copy-done = f32[4,512,128,4]{2,1,3,0:T(8,128)} copy-done((f32[4,512,128,4]{2,1,3,0:T(8,128)}, f32[4,512,128,4]{2,1,3,0:T(8,128)S(1)}, u32[]{:S(2)}) %copy-start) | copy-done | bytes 4194328 | tf_op jit(solution)/shard_map/while
  76.9 0.9 fusion.52
  78.1 4.9 %fusion.53 = f32[4,4,128,128]{3,2,1,0:T(8,128)} fusion(bf16[512,4,128,1]{0,2,3,1:T(8,128)(2,1)S(1)} %bitcast.91, f32[4,512,128,4]{2,1,3,0:T(8,128)} %copy-done, f32[4,4,128]{2,1,0:T(4,128)S(1)} %max.11, pred[512]{0:T(512)(128)(4,1)S(1)} %fusion.51, f32[4,4,128,128]{3,2,1,0:T(8,128)} %get-tuple-element.359, f32[4,4,128]{2,1,0:T(4,128)S(1)} %bitcast.107), kind=kOutput, calls=%fused_computation.11.clone.1 | convolution fusion | flops 273154048 | bytes 6832640 | tf_op jit(solution)/shard_map/while/body/eval_jaxpr/gqtb,bgd->gqtd/dot_general | solution.py:58
  83.0 1.1 constant_dynamic-slice_fusion.3
  85.0 1.1 bitcast_reduce_fusion.2
  86.1 1.9 %copy-done = f32[4,512,128,4]{2,1,3,0:T(8,128)} copy-done((f32[4,512,128,4]{2,1,3,0:T(8,128)}, f32[4,512,128,4]{2,1,3,0:T(8,128)S(1)}, u32[]{:S(2)}) %copy-start) | copy-done | bytes 4194328 | tf_op jit(solution)/shard_map/while
  89.2 4.9 %fusion.53 = f32[4,4,128,128]{3,2,1,0:T(8,128)} fusion(bf16[512,4,128,1]{0,2,3,1:T(8,128)(2,1)S(1)} %bitcast.91, f32[4,512,128,4]{2,1,3,0:T(8,128)} %copy-done, f32[4,4,128]{2,1,0:T(4,128)S(1)} %max.11, pred[512]{0:T(512)(128)(4,1)S(1)} %fusion.51, f32[4,4,128,128]{3,2,1,0:T(8,128)} %get-tuple-element.359, f32[4,4,128]{2,1,0:T(4,128)S(1)} %bitcast.107), kind=kOutput, calls=%fused_computation.11.clone.1 | convolution fusion | flops 273154048 | bytes 6832640 | tf_op jit(solution)/shard_map/while/body/eval_jaxpr/gqtb,bgd->gqtd/dot_general | solution.py:58
  94.1 1.7 %fusion.22 = (f32[128]{0:T(128)S(1)}, bf16[4,4,128,128]{3,2,1,0:T(8,128)(2,1)S(1)}) fusion(f32[4,4,128,128]{3,2,1,0:T(8,128)} %get-tuple-element.227, f32[4,4,128]{2,1,0:T(4,128)S(1)} %get-tuple-element.228), kind=kLoop, calls=%fused_computation.37 | loop fusion | flops 1310592 | bytes 1581568 | tf_op jit(solution)/shard_map/reduce_sum | solution.py:23
  97.3 1.5 %collective-permute-start = (bf16[1,128,2048]{2,1,0:T(8,128)(2,1)S(1)}, bf16[1,128,2048]{2,1,0:T(8,128)(2,1)S(1)}, u32[]{:S(2)}, u32[]{:S(2)}) collective-permute-start(bf16[1,128,2048]{2,1,0:T(8,128)(2,1)S(1)} %add_convert_fusion), channel_id=1, source_target_pairs={{0,8},{8,16},{16,24},{24,0},{1,9},{9,17},{17,25},{25,1},{2,10},{10... | collective-permute-start | bytes 1572872 | tf_op jit(solution)/shard_map/ppermute | solution.py:19
  98.8 12.8 %collective-permute-done = bf16[1,128,2048]{2,1,0:T(8,128)(2,1)S(1)} collective-permute-done((bf16[1,128,2048]{2,1,0:T(8,128)(2,1)S(1)}, bf16[1,128,2048]{2,1,0:T(8,128)(2,1)S(1)}, u32[]{:S(2)}, u32[]{:S(2)}) %collective-permute-start) | collective-permute-done | bytes 524320 | tf_op jit(solution)/shard_map/ppermute | solution.py:19
  (60 shorter events, 9.3 us)
Async XLA Ops:
  0.0 12.4 %copy-start.4 = (bf16[1,128,512]{2,1,0:T(8,128)(2,1)S(1)}, bf16[1,128,512]{2,1,0:T(8,128)(2,1)}, u32[]{:S(2)}) copy-start(bf16[1,128,512]{2,1,0:T(8,128)(2,1)} %param.13) | copy-start | bytes 393220
  0.0 12.3 %copy-start.3 = (bf16[1,128,512]{2,1,0:T(8,128)(2,1)S(1)}, bf16[1,128,512]{2,1,0:T(8,128)(2,1)}, u32[]{:S(2)}) copy-start(bf16[1,128,512]{2,1,0:T(8,128)(2,1)} %param.15) | copy-start | bytes 393220
  0.0 12.6 %copy-start.6 = (bf16[1,128,512]{2,1,0:T(8,128)(2,1)S(1)}, bf16[1,128,512]{2,1,0:T(8,128)(2,1)}, u32[]{:S(2)}) copy-start(bf16[1,128,512]{2,1,0:T(8,128)(2,1)} %param.14) | copy-start | bytes 393220
  0.0 12.5 %copy-start.5 = (bf16[1,128,512]{2,1,0:T(8,128)(2,1)S(1)}, bf16[1,128,512]{2,1,0:T(8,128)(2,1)}, u32[]{:S(2)}) copy-start(bf16[1,128,512]{2,1,0:T(8,128)(2,1)} %param.16) | copy-start | bytes 393220
  0.0 13.4 %copy-start.1 = (bf16[1,128,2048]{2,1,0:T(8,128)(2,1)S(1)}, bf16[1,128,2048]{2,1,0:T(8,128)(2,1)}, u32[]{:S(2)}) copy-start(bf16[1,128,2048]{2,1,0:T(8,128)(2,1)} %param.10) | copy-start | bytes 1572868
  0.0 14.3 %copy-start.7 = (bf16[1,2048]{1,0:T(2,128)(2,1)S(1)}, bf16[1,2048]{1,0:T(2,128)(2,1)}, u32[]{:S(2)}) copy-start(bf16[1,2048]{1,0:T(2,128)(2,1)} %param.11) | copy-start | bytes 12292
  4.3 10.6 %copy-start.8 = (bf16[1,2048]{1,0:T(2,128)(2,1)S(1)}, bf16[1,2048]{1,0:T(2,128)(2,1)}, u32[]{:S(2)}) copy-start(bf16[1,2048]{1,0:T(2,128)(2,1)} %param.12) | copy-start | bytes 12292
  5.9 32.9 %all-to-all-start = ((bf16[8,128,512]{1,2,0:T(8,128)(2,1)}), bf16[8,128,512]{1,2,0:T(8,128)(2,1)S(1)}, u32[]{:S(2)}, u32[]{:S(2)}) async-start(bf16[8,128,512]{1,2,0:T(8,128)(2,1)} %get-tuple-element.267), calls=%async_computation | async-start | bytes 2097152 | tf_op jit(solution)/shard_map/all_to_all | solution.py:97
  38.8 30.8 %all-to-all-start.1 = ((bf16[8,128,512]{1,2,0:T(8,128)(2,1)}), bf16[8,128,512]{1,2,0:T(8,128)(2,1)}, u32[]{:S(2)}, u32[]{:S(2)}) async-start(bf16[8,128,512]{1,2,0:T(8,128)(2,1)} %get-tuple-element.266), calls=%async_computation.1 | async-start | bytes 2097152 | tf_op jit(solution)/shard_map/all_to_all | solution.py:98
  75.0 1.9 %copy-start = (f32[4,512,128,4]{2,1,3,0:T(8,128)}, f32[4,512,128,4]{2,1,3,0:T(8,128)S(1)}, u32[]{:S(2)}) copy-start(f32[4,512,128,4]{2,1,3,0:T(8,128)S(1)} %get-tuple-element.339) | copy-start | bytes 12582916 | tf_op jit(solution)/shard_map/while
  86.1 1.9 %copy-start = (f32[4,512,128,4]{2,1,3,0:T(8,128)}, f32[4,512,128,4]{2,1,3,0:T(8,128)S(1)}, u32[]{:S(2)}) copy-start(f32[4,512,128,4]{2,1,3,0:T(8,128)S(1)} %get-tuple-element.339) | copy-start | bytes 12582916 | tf_op jit(solution)/shard_map/while
  94.1 3.0 %copy-start.2 = (bf16[1,128,2048]{2,1,0:T(8,128)(2,1)S(1)}, bf16[1,128,2048]{2,1,0:T(8,128)(2,1)}, u32[]{:S(2)}) copy-start(bf16[1,128,2048]{2,1,0:T(8,128)(2,1)} %param.10) | copy-start | bytes 1572868
  97.3 14.3 %collective-permute-start = (bf16[1,128,2048]{2,1,0:T(8,128)(2,1)S(1)}, bf16[1,128,2048]{2,1,0:T(8,128)(2,1)S(1)}, u32[]{:S(2)}, u32[]{:S(2)}) collective-permute-start(bf16[1,128,2048]{2,1,0:T(8,128)(2,1)S(1)} %add_convert_fusion), channel_id=1, source_target_pairs={{0,8},{8,16},{16,24},{24,0},{1,9},{9,17},{17,25},{25,1},{2,10},{10... | collective-permute-start | bytes 1572872 | tf_op jit(solution)/shard_map/ppermute | solution.py:19
where the time goes:
time: 113 us; the launch traced here: 112 us
  waiting for transfers between devices  59.5 us (53%)
  local copies, waits for them, and re-layouts  17.7 us (16%)
  matrix products  14.1 us (12%)
  starting transfers between devices  12.2 us (11%)
  other arithmetic  7.95 us (7%)
    all_to_all x1, waiting for transfers between devices, on_device(): lax.all_to_all(outgoing_keys, 'seq', split_axis=0, concat_axis=0, tiled=T...  23.6 us
    all_to_all x1, waiting for transfers between devices, on_device(): lax.all_to_all(outgoing_values, 'seq', split_axis=0, concat_axis=0, tiled...  23.1 us
    ppermute x1, waiting for transfers between devices, passed_along(): return lax.ppermute(value, axis, pairs)  12.8 us
    dot_general x3, matrix products, absorb(): jnp.einsum('gqtb,bgd->gqtd', weights.astype(jnp.bfloat16), value_block.re...  11.5 us
    all_to_all x1, starting transfers between devices, on_device(): lax.all_to_all(outgoing_keys, 'seq', split_axis=0, concat_axis=0, tiled=T...  6.38 us
    all_to_all x1, starting transfers between devices, on_device(): lax.all_to_all(outgoing_values, 'seq', split_axis=0, concat_axis=0, tiled...  4.24 us
    while x6, local copies, waits for them, and re-layouts  3.83 us
    dynamic_slice x4, local copies, waits for them, and re-layouts, one_block(): value_block = lax.dynamic_slice_in_dim(value_rows, offset, step_rows, 0)  2.64 us
  transfers between devices with their start and end apart: 3, of which 3 were waited for; matrix products, arithmetic and copies ran while one was open for 5% of the time, Pallas kernels for 0%

commit v1 on v0

v1 whole, which is shorter than its diff:
```python
import functools
import math

import jax
import jax.numpy as jnp
from jax import lax
from jax.experimental import pallas as pl
from jax.experimental.pallas import tpu as pltpu
from jax.sharding import PartitionSpec as P

HEAD = 128
EPS = 1e-06
masked_score = -1e30
MESH = pl.DeviceIdType.MESH


def kernel(
    sections,
    seq_count,
    groups,
    first_key_ref,
    hidden_ref,
    query_gain_ref,
    out_gain_ref,
    keys_now_ref,
    values_now_ref,
    keys_cached_ref,
    values_cached_ref,
    out_ref,
    now_own,
    cached_own,
    arrived,
    hidden_own,
    query_gain,
    out_gain,
    queries_t,
    highest,
    totals,
    weighted,
    attended_own,
    final_own,
    scale_own,
    hidden_in,
    gain_in,
    attended_in,
    final_in,
    scale_in,
    squares,
    local_sem,
    arrive_sem,
    chain_sem,
    partner_sem,
    section_send,
    section_recv,
):
    rows, width = hidden_ref.shape
    group_width = width // groups
    heads_in_group = group_width // HEAD
    chips = seq_count // 2
    early = group_width * (groups - 1)
    factor = math.log2(math.e) * HEAD ** (-0.5)
    section = lax.axis_index("section")
    me = lax.axis_index("seq")
    chip = lax.div(me, 2)
    core = lax.rem(me, 2)
    partner = me + 1 - 2 * core
    next_section = lax.rem(section + 1, sections)
    last_section = lax.rem(section + sections - 1, sections)
    limit = first_key_ref[0]

    hidden_copy = pltpu.make_async_copy(hidden_ref, hidden_own, local_sem.at[0])
    gain_copy = pltpu.make_async_copy(query_gain_ref, query_gain, local_sem.at[1])
    out_gain_copy = pltpu.make_async_copy(out_gain_ref, out_gain, local_sem.at[2])
    pieces = []
    for group in range(groups):
        columns = pl.ds(group * HEAD, HEAD)
        pieces.append(
            [
                pltpu.make_async_copy(
                    source.at[:, columns],
                    packed.at[group, :, pl.ds(half * HEAD, HEAD)],
                    local_sem.at[3 + 4 * group + number],
                )
                for number, (source, packed, half) in enumerate(
                    (
                        (keys_now_ref, now_own, 0),
                        (values_now_ref, now_own, 1),
                        (keys_cached_ref, cached_own, 0),
                        (values_cached_ref, cached_own, 1),
                    )
                )
            ]
        )
    for copy in pieces[0]:
        copy.start()
    hidden_copy.start()
    gain_copy.start()
    out_gain_copy.start()
    for group in range(1, groups):
        for copy in pieces[group]:
            copy.start()

    barrier = pltpu.get_barrier_semaphore()

    def greet(section_id, seq_id):
        pl.semaphore_signal(barrier, inc=1, device_id=(section_id, seq_id), device_id_type=MESH)

    greet(section, partner)
    greet(next_section, me)
    greet(last_section, me)

    @pl.when(chip > 0)
    def _():
        greet(section, me - 2)

    @pl.when(chip < chips - 1)
    def _():
        greet(section, me + 2)

    ends = (chip == 0).astype(jnp.int32) + (chip == chips - 1).astype(jnp.int32)
    pl.semaphore_wait(barrier, 5 - ends)

    def along(source, owner, group, send_sem, target):
        return pltpu.make_async_remote_copy(
            src_ref=source,
            dst_ref=arrived.at[owner, group],
            send_sem=send_sem,
            recv_sem=arrive_sem.at[owner, group],
            device_id=(section, target),
            device_id_type=MESH,
        )

    def to_next(source, target, number):
        return pltpu.make_async_remote_copy(
            src_ref=source,
            dst_ref=target,
            send_sem=section_send.at[number],
            recv_sem=section_recv.at[number],
            device_id=(next_section, me),
            device_id_type=MESH,
        )

    hidden_send = to_next(hidden_ref.at[:, pl.ds(0, early)], hidden_in, groups)
    gain_send = to_next(out_gain, gain_in, groups + 1)
    scale_send = to_next(scale_own, scale_in, groups + 2)
    final_send = to_next(final_own, final_in, groups - 1)

    def attended_send(group):
        return to_next(attended_own.at[group], attended_in.at[group], group)

    for group in range(groups):
        for copy in pieces[group]:
            copy.wait()

        @pl.when(chip < chips - 1)
        def _():
            along(now_own.at[group], me, group, chain_sem.at[chip, group], me + 2).start()

        @pl.when(chip > 0)
        def _():
            along(cached_own.at[group], me, group, chain_sem.at[chips, group], me - 2).start()

        @pl.when(core == 0)
        def _():
            along(now_own.at[group], me, group, partner_sem.at[chip, group], partner).start()

        @pl.when(core == 1)
        def _():
            along(cached_own.at[group], me, group, partner_sem.at[chip, group], partner).start()

        if group == 0:
            hidden_send.start()
            out_gain_copy.wait()
            gain_send.start()

    hidden_copy.wait()
    gain_copy.wait()
    widened = hidden_own[...].astype(jnp.float32)
    scale = lax.rsqrt(jnp.mean(widened * widened, axis=-1, keepdims=True) + EPS)
    for head in range(groups * heads_in_group):
        columns = slice(head * HEAD, (head + 1) * HEAD)
        queries = (
            hidden_own[:, columns].astype(jnp.float32)
            * scale
            * query_gain[:, columns].astype(jnp.float32)
        )
        place = head % heads_in_group
        queries_t[head // heads_in_group, :, place * rows : (place + 1) * rows] = (
            queries.T.astype(jnp.bfloat16)
        )

    def scored(keys, group):
        return jnp.dot(keys, queries_t[group], preferred_element_type=jnp.float32)

    def summed(values, weights):
        return lax.dot_general(
            values,
            weights.astype(jnp.bfloat16),
            (((0,), (0,)), ((), ())),
            preferred_element_type=jnp.float32,
        )

    def absorb(scores, values, group):
        old = highest[group]
        new = jnp.maximum(old, jnp.max(scores, axis=0, keepdims=True))
        rescale = jnp.exp2((old - new) * factor)
        weights = jnp.exp2((scores - new) * factor)
        highest[group] = new
        totals[group] = totals[group] * rescale + jnp.sum(weights, axis=0, keepdims=True)
        weighted[group] = weighted[group] * rescale + summed(values, weights)

    def own_part(group, _):
        key_pos = lax.broadcasted_iota(jnp.int32, (rows, group_width // HEAD * rows), 0)
        query_pos = lax.rem(
            lax.broadcasted_iota(jnp.int32, (rows, group_width // HEAD * rows), 1), rows
        )
        scores = jnp.where(
            key_pos <= query_pos, scored(now_own[group, :, :HEAD], group), masked_score
        )
        new = jnp.max(scores, axis=0, keepdims=True)
        weights = jnp.exp2((scores - new) * factor)
        highest[group] = new
        totals[group] = jnp.sum(weights, axis=0, keepdims=True)
        weighted[group] = summed(now_own[group, :, HEAD:], weights)
        scores = jnp.where(
            (key_pos > query_pos) & (key_pos + me * rows >= limit),
            scored(cached_own[group, :, :HEAD], group),
            masked_score,
        )
        absorb(scores, cached_own[group, :, HEAD:], group)
        along(arrived.at[partner, group], partner, group, partner_sem.at[chip, group], partner).wait_recv()
        bound = jnp.where(partner > me, limit, 0)
        scores = jnp.where(
            key_pos + partner * rows >= bound,
            scored(arrived[partner, group, :, :HEAD], group),
            masked_score,
        )
        absorb(scores, arrived[partner, group, :, HEAD:], group)
        return 0

    lax.fori_loop(0, groups, own_part, 0)

    others = chips - 1
    both = jnp.minimum(chip, others - chip)

    def visited(step):
        group = lax.div(step, others)
        order = lax.rem(step, others) + 1
        paired = order <= 2 * both
        distance = jnp.where(paired, lax.div(order + 1, 2), order - both)
        lower = jnp.where(paired, lax.rem(order, 2) == 1, chip > both)
        return group, chip + jnp.where(lower, -distance, distance), lower

    def relay(step):
        group, other, lower = visited(step)
        owner = 2 * other + core
        block = arrived.at[owner, group]
        along(block, owner, group, chain_sem.at[other, group], partner).wait_recv()

        @pl.when(lower & (chip < chips - 1))
        def _():
            along(block, owner, group, chain_sem.at[other, group], me + 2).start()

        @pl.when(jnp.logical_not(lower) & (chip > 0))
        def _():
            along(block, owner, group, chain_sem.at[other, group], me - 2).start()

        along(block, owner, group, partner_sem.at[other, group], partner).start()

    def fold(step):
        group, other, lower = visited(step)
        owner = 2 * other + 1 - core
        block = arrived.at[owner, group]
        along(block, owner, group, chain_sem.at[other, group], partner).wait_recv()
        first = pl.multiple_of(2 * other, 2)
        both_blocks = arrived[pl.ds(first, 2), group].reshape(2 * rows, 2 * HEAD)
        key_pos = lax.broadcasted_iota(jnp.int32, (2 * rows, 1), 0) + first * rows
        bound = jnp.where(lower, 0, limit)
        scores = jnp.where(key_pos >= bound, scored(both_blocks[:, :HEAD], group), masked_score)
        absorb(scores, both_blocks[:, HEAD:], group)

    squares[...] = jnp.zeros_like(squares)

    def closed(group):
        attended_t = (weighted[group] / totals[group]).astype(jnp.bfloat16).astype(jnp.float32)
        row_squares = jnp.sum(attended_t * attended_t, axis=0, keepdims=True)
        for head in range(heads_in_group):
            squares[...] += row_squares[:, head * rows : (head + 1) * rows]
        return [
            attended_t[:, head * rows : (head + 1) * rows].T for head in range(heads_in_group)
        ]

    def one_step(step, _):
        relay(step)
        fold(step - 1)
        group = lax.div(step, others)

        @pl.when(lax.rem(step, others) == 0)
        def _():
            for head, value in enumerate(closed(group - 1)):
                attended_own[group - 1, :, head * HEAD : (head + 1) * HEAD] = value.astype(
                    jnp.bfloat16
                )
            attended_send(group - 1).start()

        return 0

    steps = groups * others
    relay(0)
    lax.fori_loop(1, steps, one_step, 0)
    fold(steps - 1)

    last = closed(groups - 1)
    row_scale = lax.rsqrt(squares[...] * (1.0 / width) + EPS)
    scale_own[...] = jnp.broadcast_to(row_scale, scale_own.shape)
    scale_send.start()
    row_scale = jnp.broadcast_to(row_scale, (HEAD, rows)).T
    for head, value in enumerate(last):
        columns = slice(early + head * HEAD, early + (head + 1) * HEAD)
        branch = value * row_scale * out_gain[:, columns].astype(jnp.float32)
        final_own[:, head * HEAD : (head + 1) * HEAD] = (
            hidden_own[:, columns].astype(jnp.float32) + branch
        ).astype(jnp.bfloat16)
    final_send.start()

    hidden_send.wait_recv()
    gain_send.wait_recv()
    for group in range(groups - 1):
        attended_send(group).wait_recv()
    scale_send.wait_recv()
    row_scale = jnp.broadcast_to(scale_in[0:1, :], (HEAD, rows)).T
    for group in range(groups - 1):
        for head in range(heads_in_group):
            start = group * group_width + head * HEAD
            columns = slice(start, start + HEAD)
            branch = (
                attended_in[group, :, head * HEAD : (head + 1) * HEAD].astype(jnp.float32)
                * row_scale
                * gain_in[:, columns].astype(jnp.float32)
            )
            out_ref[:, columns] = (
                hidden_in[:, columns].astype(jnp.float32) + branch
            ).astype(jnp.bfloat16)
    final_send.wait_recv()
    out_ref[:, early:] = final_in[...]

    hidden_send.wait_send()
    gain_send.wait_send()
    scale_send.wait_send()
    final_send.wait_send()
    for group in range(groups - 1):
        attended_send(group).wait_send()

    def drained(step, _):
        group, other, lower = visited(step)
        owner = 2 * other + core
        block = arrived.at[owner, group]

        @pl.when((lower & (chip < chips - 1)) | (jnp.logical_not(lower) & (chip > 0)))
        def _():
            along(block, owner, group, chain_sem.at[other, group], partner).wait_send()

        along(block, owner, group, partner_sem.at[other, group], partner).wait_send()
        return 0

    lax.fori_loop(0, steps, drained, 0)
    for group in range(groups):

        @pl.when(chip < chips - 1)
        def _():
            along(now_own.at[group], me, group, chain_sem.at[chip, group], partner).wait_send()

        @pl.when(chip > 0)
        def _():
            along(cached_own.at[group], me, group, chain_sem.at[chips, group], partner).wait_send()

        along(now_own.at[group], me, group, partner_sem.at[chip, group], partner).wait_send()


def solution(mesh):
    sections, seq_count = mesh.shape["section"], mesh.shape["seq"]

    def on_device(
        hidden, query_gain, out_gain, keys_now, values_now, keys_cached, values_cached, first_key
    ):
        _, rows, width = hidden.shape
        groups = keys_now.shape[-1] // HEAD
        group_width = width // groups
        query_rows = group_width // HEAD * rows
        chips = seq_count // 2
        half, full = jnp.bfloat16, jnp.float32
        anywhere = pl.BlockSpec(memory_space=pl.ANY)
        result = pl.pallas_call(
            functools.partial(kernel, sections, seq_count, groups),
            out_shape=jax.ShapeDtypeStruct((rows, width), half),
            in_specs=[pl.BlockSpec(memory_space=pltpu.SMEM)] + [anywhere] * 7,
            out_specs=pl.BlockSpec(memory_space=pltpu.VMEM),
            scratch_shapes=[
                pltpu.VMEM((groups, rows, 2 * HEAD), half),
                pltpu.VMEM((groups, rows, 2 * HEAD), half),
                pltpu.VMEM((seq_count, groups, rows, 2 * HEAD), half),
                pltpu.VMEM((rows, width), half),
                pltpu.VMEM((1, width), half),
                pltpu.VMEM((1, width), half),
                pltpu.VMEM((groups, HEAD, query_rows), half),
                pltpu.VMEM((groups, 1, query_rows), full),
                pltpu.VMEM((groups, 1, query_rows), full),
                pltpu.VMEM((groups, HEAD, query_rows), full),
                pltpu.VMEM((groups - 1, rows, group_width), half),
                pltpu.VMEM((rows, group_width), half),
                pltpu.VMEM((8, rows), full),
                pltpu.VMEM((rows, width - group_width), half),
                pltpu.VMEM((1, width), half),
                pltpu.VMEM((groups - 1, rows, group_width), half),
                pltpu.VMEM((rows, group_width), half),
                pltpu.VMEM((8, rows), full),
                pltpu.VMEM((1, rows), full),
                pltpu.SemaphoreType.DMA((3 + 4 * groups,)),
                pltpu.SemaphoreType.DMA((seq_count, groups)),
                pltpu.SemaphoreType.DMA((chips + 1, groups)),
                pltpu.SemaphoreType.DMA((chips, groups)),
                pltpu.SemaphoreType.DMA((groups + 3,)),
                pltpu.SemaphoreType.DMA((groups + 3,)),
            ],
            compiler_params=pltpu.CompilerParams(collective_id=0, has_side_effects=True),
        )(
            first_key,
            hidden[0],
            query_gain,
            out_gain,
            keys_now[0],
            values_now[0],
            keys_cached[0],
            values_cached[0],
        )
        return result[None]

    return jax.shard_map(
        on_device,
        mesh=mesh,
        in_specs=(
            P("section", "seq", None),
            P("section", None),
            P("section", None),
            P("section", "seq", None),
            P("section", "seq", None),
            P("section", "seq", None),
            P("section", "seq", None),
            P("section"),
        ),
        out_specs=P("section", "seq", None),
        check_vma=False,
    )
```

time: 113 us -> 42.2 us (0.37)
  waiting for transfers between devices: 59.5 us -> 0 us
  Pallas kernels: 0 us -> 39.5 us
  local copies, waits for them, and re-layouts: 17.7 us -> 1.88 us
  matrix products: 14.1 us -> 0 us
  starting transfers between devices: 12.2 us -> 0 us
  other arithmetic: 7.95 us -> 0 us
    all_to_all x2 -> x0, waiting for transfers between devices: 46.7 us -> none  [the longest x1 23.6 us: on_device(): lax.all_to_all(outgoing_keys, 'seq', split_axis=0, concat_axis=0, tiled=T...]
    pallas_call x0 -> x1, Pallas kernels: none -> 39.5 us  [on_device(): pl.pallas_call(functools.partial(kernel, sections, seq_count, groups), ou...]
    dot_general x6 -> x0, matrix products: 14.1 us -> none  [the longest x3 11.5 us: absorb(): jnp.einsum('gqtb,bgd->gqtd', weights.astype(jnp.bfloat16), value_block.re...]
    ppermute x1 -> x0, waiting for transfers between devices: 12.8 us -> none  [passed_along(): return lax.ppermute(value, axis, pairs)]
    all_to_all x2 -> x0, starting transfers between devices: 10.6 us -> none  [the longest x1 6.38 us: on_device(): lax.all_to_all(outgoing_keys, 'seq', split_axis=0, concat_axis=0, tiled=T...]
    broadcast_in_dim x4 -> x0, local copies, waits for them, and re-layouts: 4.18 us -> none  [the longest x2 2.13 us: on_device(): outgoing_keys = jnp.where(target, keys_now[0][None], keys_cached[0][None])]
    reduce_sum x5 -> x0, other arithmetic: 4.1 us -> none  [the longest x3 2.21 us: absorb(): totals = totals * rescale + jnp.sum(weights, axis=-1)]
    while x6 -> x0, local copies, waits for them, and re-layouts: 3.83 us -> none
  transfers between devices with their start and end apart: 3 -> 0, of which waited for: 3 -> 0; matrix products, arithmetic and copies ran while one was open for 5% -> 0% of each run, Pallas kernels for 0% -> 0%
where the time goes in v1:
time: 42.2 us; the launch traced here: 42.1 us
  Pallas kernels  39.5 us (94%)
  local copies, waits for them, and re-layouts  1.88 us (4%)
  between operations  0.66 us (2%)
    pallas_call x1, Pallas kernels, on_device(): pl.pallas_call(functools.partial(kernel, sections, seq_count, groups), ou...  39.5 us
    unnamed x1, local copies, waits for them, and re-layouts  1.88 us

profile of v1, /device:TPU:0, one launch (start us, length us, event | category | flops | bytes accessed | tf_op | source)
XLA Modules:
  0.0 42.1 jit_solution(14655196184197365334)
XLA Ops:
  0.7 39.5 %shard_map.82 = bf16[128,2048]{1,0:T(8,128)(2,1)} custom-call(s32[1]{0:T(128)S(6)} %copy.10.first_key_ref, bf16[128,2048]{1,0:T(8,128)(2,1)} %bitcast.7, bf16[1,2048]{1,0:T(2,128)(2,1)} %query_gain_ref.1, bf16[1,2048]{1,0:T(2,128)(2,1)} %out_gain_ref.1, bf16[128,512]{1,0:T(8,128)(2,1)} %bitcast.8, bf16[128,512]{1,0:T(8,128)(2,1)} %bitcast.9, ...), custom_call_target="tpu_custom_call" | custom-call | tf_op jit(solution)/shard_map/pallas_call | solution.py:393
  40.2 1.9 %copy.11 = bf16[1,128,2048]{2,1,0:T(8,128)(2,1)} copy(bf16[1,128,2048]{2,1,0:T(8,128)(2,1)} %bitcast.6) | data formatting | bytes 1048576

commit v2 on v1

--- a/solution.py
+++ b/solution.py
@@ -10,6 +10,8 @@
 
 HEAD = 128
 EPS = 1e-06
+AHEAD = 2
+ROOM = 20 << 20
 masked_score = -1e30
 MESH = pl.DeviceIdType.MESH
 
@@ -244,15 +246,16 @@
     both = jnp.minimum(chip, others - chip)
 
     def visited(step):
-        group = lax.div(step, others)
-        order = lax.rem(step, others) + 1
+        shared = step < 2 * others
+        group = jnp.where(shared, lax.rem(step, 2), lax.div(step, others))
+        order = jnp.where(shared, lax.div(step, 2), lax.rem(step, others)) + 1
         paired = order <= 2 * both
         distance = jnp.where(paired, lax.div(order + 1, 2), order - both)
         lower = jnp.where(paired, lax.rem(order, 2) == 1, chip > both)
-        return group, chip + jnp.where(lower, -distance, distance), lower
+        return group, chip + jnp.where(lower, -distance, distance), lower, order
 
     def relay(step):
-        group, other, lower = visited(step)
+        group, other, lower, order = visited(step)
         owner = 2 * other + core
         block = arrived.at[owner, group]
         along(block, owner, group, chain_sem.at[other, group], partner).wait_recv()
@@ -268,7 +271,7 @@
         along(block, owner, group, partner_sem.at[other, group], partner).start()
 
     def fold(step):
-        group, other, lower = visited(step)
+        group, other, lower, order = visited(step)
         owner = 2 * other + 1 - core
         block = arrived.at[owner, group]
         along(block, owner, group, chain_sem.at[other, group], partner).wait_recv()
@@ -282,7 +285,7 @@
     squares[...] = jnp.zeros_like(squares)
 
     def closed(group):
-        attended_t = (weighted[group] / totals[group]).astype(jnp.bfloat16).astype(jnp.float32)
+        attended_t = (weighted[group] * (1.0 / totals[group])).astype(jnp.bfloat16).astype(jnp.float32)
         row_squares = jnp.sum(attended_t * attended_t, axis=0, keepdims=True)
         for head in range(heads_in_group):
             squares[...] += row_squares[:, head * rows : (head + 1) * rows]
@@ -290,24 +293,30 @@
             attended_t[:, head * rows : (head + 1) * rows].T for head in range(heads_in_group)
         ]
 
-    def one_step(step, _):
-        relay(step)
-        fold(step - 1)
-        group = lax.div(step, others)
-
-        @pl.when(lax.rem(step, others) == 0)
-        def _():
-            for head, value in enumerate(closed(group - 1)):
-                attended_own[group - 1, :, head * HEAD : (head + 1) * HEAD] = value.astype(
+    def fold_and_send(step):
+        fold(step)
+        group, _, _, order = visited(step)
+
+        @pl.when((order == others) & (group < groups - 1))
+        def _():
+            for head, value in enumerate(closed(group)):
+                attended_own[group, :, head * HEAD : (head + 1) * HEAD] = value.astype(
                     jnp.bfloat16
                 )
-            attended_send(group - 1).start()
-
+            attended_send(group).start()
+
+    def one_step(step, _):
+        @pl.when(step < steps)
+        def _():
+            relay(step)
+
+        fold_and_send(step - AHEAD)
         return 0
 
     steps = groups * others
-    relay(0)
-    lax.fori_loop(1, steps, one_step, 0)
+    for step in range(AHEAD):
+        relay(step)
+    lax.fori_loop(AHEAD, steps + AHEAD - 1, one_step, 0)
     fold(steps - 1)
 
     last = closed(groups - 1)
@@ -352,7 +361,7 @@
         attended_send(group).wait_send()
 
     def drained(step, _):
-        group, other, lower = visited(step)
+        group, other, lower, order = visited(step)
         owner = 2 * other + core
         block = arrived.at[owner, group]
 
@@ -389,6 +398,7 @@
         query_rows = group_width // HEAD * rows
         chips = seq_count // 2
         half, full = jnp.bfloat16, jnp.float32
+        arrived_bytes = seq_count * rows * keys_now.shape[-1] * 4
         anywhere = pl.BlockSpec(memory_space=pl.ANY)
         result = pl.pallas_call(
             functools.partial(kernel, sections, seq_count, groups),
@@ -422,16 +432,21 @@
                 pltpu.SemaphoreType.DMA((groups + 3,)),
                 pltpu.SemaphoreType.DMA((groups + 3,)),
             ],
-            compiler_params=pltpu.CompilerParams(collective_id=0, has_side_effects=True),
+            compiler_params=pltpu.CompilerParams(collective_id=0, has_side_effects=True, vmem_limit_bytes=arrived_bytes + ROOM),
         )(
             first_key,
-            hidden[0],
-            query_gain,
-            out_gain,
-            keys_now[0],
-            values_now[0],
-            keys_cached[0],
-            values_cached[0],
+            *(
+                pltpu.with_memory_space_constraint(value, pltpu.HBM)
+                for value in (
+                    hidden[0],
+                    query_gain,
+                    out_gain,
+                    keys_now[0],
+                    values_now[0],
+                    keys_cached[0],
+                    values_cached[0],
+                )
+            ),
         )
         return result[None]
 

time: 42.2 us -> 36.3 us (0.86)
  Pallas kernels: 39.5 us -> 34.7 us
  local copies, waits for them, and re-layouts: 1.88 us -> 0.8 us
    pallas_call x1, Pallas kernels: 39.5 us -> 34.7 us  [on_device(): pl.pallas_call(functools.partial(kernel, sections, seq_count, groups), ou...]
    unnamed x1, local copies, waits for them, and re-layouts: 1.88 us -> 0.8 us
where the time goes in v2:
time: 36.3 us; the launch traced here: 36.2 us
  Pallas kernels  34.7 us (96%)
  local copies, waits for them, and re-layouts  0.8 us (2%)
  between operations  0.66 us (2%)
    pallas_call x1, Pallas kernels, on_device(): pl.pallas_call(functools.partial(kernel, sections, seq_count, groups), ou...  34.7 us
    unnamed x1, local copies, waits for them, and re-layouts  0.8 us

profile of v2, /device:TPU:0, one launch (start us, length us, event | category | flops | bytes accessed | tf_op | source)
XLA Modules:
  0.0 36.2 jit_solution(487238495130747334)
XLA Ops:
  0.7 34.7 %shard_map.82 = bf16[128,2048]{1,0:T(8,128)(2,1)S(1)} custom-call(s32[1]{0:T(128)S(6)} %copy.10.first_key_ref, bf16[128,2048]{1,0:T(8,128)(2,1)} %bitcast.7, bf16[1,2048]{1,0:T(2,128)(2,1)} %query_gain_ref.1, bf16[1,2048]{1,0:T(2,128)(2,1)} %out_gain_ref.1, bf16[128,512]{1,0:T(8,128)(2,1)} %bitcast.8, bf16[128,512]{1,0:T(8,128)(2,1)} %bitcast.9, ...), custom_call_target="tpu_custom_call" | custom-call | tf_op jit(solution)/shard_map/pallas_call | solution.py:403
  35.4 0.8 %copy.11 = bf16[1,128,2048]{2,1,0:T(8,128)(2,1)} copy(bf16[1,128,2048]{2,1,0:T(8,128)(2,1)S(1)} %bitcast.6) | data formatting | bytes 1048576

commit v3 on v2

--- a/solution.py
+++ b/solution.py
@@ -70,6 +70,23 @@
     last_section = lax.rem(section + sections - 1, sections)
     limit = first_key_ref[0]
 
+    barrier = pltpu.get_barrier_semaphore()
+
+    def greet(section_id, seq_id):
+        pl.semaphore_signal(barrier, inc=1, device_id=(section_id, seq_id), device_id_type=MESH)
+
+    greet(section, partner)
+    greet(next_section, me)
+    greet(last_section, me)
+
+    @pl.when(chip > 0)
+    def _():
+        greet(section, me - 2)
+
+    @pl.when(chip < chips - 1)
+    def _():
+        greet(section, me + 2)
+
     hidden_copy = pltpu.make_async_copy(hidden_ref, hidden_own, local_sem.at[0])
     gain_copy = pltpu.make_async_copy(query_gain_ref, query_gain, local_sem.at[1])
     out_gain_copy = pltpu.make_async_copy(out_gain_ref, out_gain, local_sem.at[2])
@@ -102,23 +119,6 @@
         for copy in pieces[group]:
             copy.start()
 
-    barrier = pltpu.get_barrier_semaphore()
-
-    def greet(section_id, seq_id):
-        pl.semaphore_signal(barrier, inc=1, device_id=(section_id, seq_id), device_id_type=MESH)
-
-    greet(section, partner)
-    greet(next_section, me)
-    greet(last_section, me)
-
-    @pl.when(chip > 0)
-    def _():
-        greet(section, me - 2)
-
-    @pl.when(chip < chips - 1)
-    def _():
-        greet(section, me + 2)
-
     ends = (chip == 0).astype(jnp.int32) + (chip == chips - 1).astype(jnp.int32)
     pl.semaphore_wait(barrier, 5 - ends)
 
@@ -142,10 +142,12 @@
             device_id_type=MESH,
         )
 
-    hidden_send = to_next(hidden_ref.at[:, pl.ds(0, early)], hidden_in, groups)
-    gain_send = to_next(out_gain, gain_in, groups + 1)
-    scale_send = to_next(scale_own, scale_in, groups + 2)
-    final_send = to_next(final_own, final_in, groups - 1)
+    hidden_send = to_next(hidden_ref.at[:, pl.ds(0, early)], hidden_in, groups - 1)
+    gain_send = to_next(out_gain, gain_in, groups)
+    scale_send = to_next(scale_own, scale_in, groups + 1)
+
+    def final_send(head):
+        return to_next(final_own.at[head], final_in.at[head], groups + 2 + head)
 
     def attended_send(group):
         return to_next(attended_own.at[group], attended_in.at[group], group)
@@ -327,10 +329,10 @@
     for head, value in enumerate(last):
         columns = slice(early + head * HEAD, early + (head + 1) * HEAD)
         branch = value * row_scale * out_gain[:, columns].astype(jnp.float32)
-        final_own[:, head * HEAD : (head + 1) * HEAD] = (
+        final_own[head] = (
             hidden_own[:, columns].astype(jnp.float32) + branch
         ).astype(jnp.bfloat16)
-    final_send.start()
+        final_send(head).start()
 
     hidden_send.wait_recv()
     gain_send.wait_recv()
@@ -350,13 +352,9 @@
             out_ref[:, columns] = (
                 hidden_in[:, columns].astype(jnp.float32) + branch
             ).astype(jnp.bfloat16)
-    final_send.wait_recv()
-    out_ref[:, early:] = final_in[...]
-
     hidden_send.wait_send()
     gain_send.wait_send()
     scale_send.wait_send()
-    final_send.wait_send()
     for group in range(groups - 1):
         attended_send(group).wait_send()
 
@@ -384,6 +382,12 @@
             along(cached_own.at[group], me, group, chain_sem.at[chips, group], partner).wait_send()
 
         along(now_own.at[group], me, group, partner_sem.at[chip, group], partner).wait_send()
+
+    for head in range(heads_in_group):
+        final_send(head).wait_recv()
+        out_ref[:, early + head * HEAD : early + (head + 1) * HEAD] = final_in[head]
+    for head in range(heads_in_group):
+        final_send(head).wait_send()
 
 
 def solution(mesh):
@@ -417,20 +421,20 @@
                 pltpu.VMEM((groups, 1, query_rows), full),
                 pltpu.VMEM((groups, HEAD, query_rows), full),
                 pltpu.VMEM((groups - 1, rows, group_width), half),
-                pltpu.VMEM((rows, group_width), half),
+                pltpu.VMEM((group_width // HEAD, rows, HEAD), half),
                 pltpu.VMEM((8, rows), full),
                 pltpu.VMEM((rows, width - group_width), half),
                 pltpu.VMEM((1, width), half),
                 pltpu.VMEM((groups - 1, rows, group_width), half),
-                pltpu.VMEM((rows, group_width), half),
+                pltpu.VMEM((group_width // HEAD, rows, HEAD), half),
                 pltpu.VMEM((8, rows), full),
                 pltpu.VMEM((1, rows), full),
                 pltpu.SemaphoreType.DMA((3 + 4 * groups,)),
                 pltpu.SemaphoreType.DMA((seq_count, groups)),
                 pltpu.SemaphoreType.DMA((chips + 1, groups)),
                 pltpu.SemaphoreType.DMA((chips, groups)),
-                pltpu.SemaphoreType.DMA((groups + 3,)),
-                pltpu.SemaphoreType.DMA((groups + 3,)),
+                pltpu.SemaphoreType.DMA((groups + 2 + group_width // HEAD,)),
+                pltpu.SemaphoreType.DMA((groups + 2 + group_width // HEAD,)),
             ],
             compiler_params=pltpu.CompilerParams(collective_id=0, has_side_effects=True, vmem_limit_bytes=arrived_bytes + ROOM),
         )(

time: 36.3 us -> 36 us (level)
  no operation moved by 1% of the time
where the time goes in v3:
time: 36 us; the launch traced here: 35.9 us
  Pallas kernels  34.4 us (96%)
  local copies, waits for them, and re-layouts  0.8 us (2%)
  between operations  0.66 us (2%)
    pallas_call x1, Pallas kernels, on_device(): pl.pallas_call(functools.partial(kernel, sections, seq_count, groups), ou...  34.4 us
    unnamed x1, local copies, waits for them, and re-layouts  0.8 us

profile of v3, /device:TPU:0, one launch (start us, length us, event | category | flops | bytes accessed | tf_op | source)
XLA Modules:
  0.0 35.9 jit_solution(6693921197365122734)
XLA Ops:
  0.7 34.4 %shard_map.82 = bf16[128,2048]{1,0:T(8,128)(2,1)S(1)} custom-call(s32[1]{0:T(128)S(6)} %copy.10.first_key_ref, bf16[128,2048]{1,0:T(8,128)(2,1)} %bitcast.7, bf16[1,2048]{1,0:T(2,128)(2,1)} %query_gain_ref.1, bf16[1,2048]{1,0:T(2,128)(2,1)} %out_gain_ref.1, bf16[128,512]{1,0:T(8,128)(2,1)} %bitcast.8, bf16[128,512]{1,0:T(8,128)(2,1)} %bitcast.9, ...), custom_call_target="tpu_custom_call" | custom-call | tf_op jit(solution)/shard_map/pallas_call | solution.py:407
  35.1 0.8 %copy.11 = bf16[1,128,2048]{2,1,0:T(8,128)(2,1)} copy(bf16[1,128,2048]{2,1,0:T(8,128)(2,1)S(1)} %bitcast.6) | data formatting | bytes 1048576
